TPU v7x, 512 devices: a whole 4x8x8 slice. The times are simulated.
512 devices in a mesh: dp: 8 (over x, core), ctx: 64 (over y, z).
Axes of the slice: x: 4, y: 8, z: 8, core: 2. Of those that a mesh axis runs over, the one named last changes fastest.
Arguments:
- queries: bfloat16 [16, 4096, 2048], P('dp', 'ctx'), may hold values from -52 to 52
- key_rows: bfloat16 [16, 4096, 2048], P('dp', 'ctx'), may hold values from -4 to 4
- value_rows: bfloat16 [16, 4096, 2048], P('dp', 'ctx'), may hold values from -6 to 6
- out_grad: bfloat16 [16, 4096, 2048], P('dp', 'ctx'), may hold values from -64 to 64
- level_slope: float32 [16], replicated, may hold values from -0.5 to 0.5
Outputs:
- query_grad: bfloat16 [16, 4096, 2048], P('dp', 'ctx')
- key_grad: bfloat16 [16, 4096, 2048], P('dp', 'ctx')
- value_grad: bfloat16 [16, 4096, 2048], P('dp', 'ctx')
- slope_grad: float32 [16], replicated
All inputs are finite; a program needn't handle non-finite values.
Results may differ from a plain program's by a relative error of at most 0.0075.
Values may be sent and summed in bfloat16 or wider, within the bound.
A program may use at most 64 MiB of HBM per device.

v0:
```python
import math

import jax
import jax.numpy as jnp
from jax import lax
from jax.sharding import PartitionSpec as P


def as_sent(x):
    return jax.tree.map(lambda a: a.astype(jnp.bfloat16) if a.dtype == jnp.float32 else a, x)


def from_partner(value, axis, apart):
    mask = 2**apart
    pairs = [(source, source ^ mask) for source in range(lax.axis_size(axis))]
    return lax.ppermute(value, axis, pairs)


def pair_mean(cells):
    shaped = cells.reshape(cells.shape[:-2] + (cells.shape[-2] // 2, 2, cells.shape[-1])).astype(
        jnp.float32
    )
    return ((shaped[..., 0, :] + shaped[..., 1, :]) * 0.5).astype(jnp.bfloat16)


def merge_level(own_pair, other_pair, flag):
    merged = []
    for own_part, other_part in zip(own_pair, other_pair):
        own_small = pair_mean(own_part)
        other_small = pair_mean(other_part)
        merged.append(
            jnp.where(
                flag == 1,
                jnp.concatenate([other_small, own_small], axis=1),
                jnp.concatenate([own_small, other_small], axis=1),
            )
        )
    return tuple(merged)


def to_heads(rows, heads):
    seqs, count, width = rows.shape
    return jnp.transpose(rows.reshape(seqs, count, heads, width // heads), (0, 2, 1, 3))


def from_heads(split):
    seqs, heads, count, head = split.shape
    return jnp.transpose(split, (0, 2, 1, 3)).reshape(seqs, count, heads * head)


def product(form, left, right):
    return jnp.einsum(form, left, right, preferred_element_type=jnp.float32)


def attend(query_four, key_four, value_four, grad_four, level_slope, block):
    head = query_four.shape[3]
    key_count = key_four.shape[2]
    scale = 1.0 / math.sqrt(head)
    column = jnp.arange(key_count, dtype=jnp.int32)
    level_of = column // block - 1
    sibling = jnp.maximum(level_of, 0)
    multiple = jnp.where(level_of < 0, 1.0, jnp.exp2(sibling.astype(jnp.float32)))
    bias = level_slope[:, None] * sibling.astype(jnp.float32)[None, :]
    raw = product("shqd,shkd->shqk", query_four, key_four)
    scores = raw * scale + bias[None, :, None, :]
    top = jnp.max(scores, axis=-1, keepdims=True)
    weights = multiple[None, None, None, :] * jnp.exp(scores - top)
    probs = weights / jnp.sum(weights, axis=-1, keepdims=True)
    probs_low = probs.astype(jnp.bfloat16)
    output = product("shqk,shkd->shqd", probs_low, value_four)
    delta = jnp.sum(grad_four.astype(jnp.float32) * output, axis=-1)
    upstream = product("shqd,shkd->shqk", grad_four, value_four)
    dscore = probs * (upstream - delta[..., None])
    slope_part = jnp.sum(dscore * sibling.astype(jnp.float32)[None, None, None, :], axis=(0, 2, 3))
    dscore_low = dscore.astype(jnp.bfloat16)
    query_part = product("shqk,shkd->shqd", dscore_low, key_four) * scale
    key_part = product("shqk,shqd->shkd", dscore_low, query_four) * scale
    value_part = product("shqk,shqd->shkd", probs_low, grad_four)
    return (query_part, key_part, value_part, slope_part)


def split_level(grad_now, direct, flag, level, block):
    half = block // 2
    lower_src = grad_now[:, :, :half]
    upper_src = grad_now[:, :, half:]
    own_src = jnp.where(flag == 1, upper_src, lower_src)
    other_src = jnp.where(flag == 1, lower_src, upper_src)
    own_half = jnp.repeat(own_src, 2, axis=2) * 0.5
    other_half = jnp.repeat(other_src, 2, axis=2) * 0.5
    sent = (other_half + direct[:, :, (level + 1) * block : (level + 2) * block]).astype(
        jnp.bfloat16
    )
    return (own_half, sent)


def shards(queries, key_rows, value_rows, out_grad, level_slope):
    seqs, block, width = queries.shape
    heads = level_slope.shape[0]
    ctx_count = lax.axis_size("ctx")
    levels = ctx_count.bit_length() - 1
    position = lax.axis_index("ctx")
    bit_list = [position // 2**level % 2 for level in range(levels)]
    own_pair = (key_rows, value_rows)
    partners = []
    for level in range(levels - 2):
        other_pair = jax.tree.map(
            lambda part, own: part.astype(own.dtype),
            from_partner(as_sent(own_pair), "ctx", level),
            own_pair,
        )
        partners.append(other_pair)
        own_pair = merge_level(own_pair, other_pair, bit_list[level])
    for level in range(levels - 2, levels):
        other_pair = jax.tree.map(
            lambda part, own: part.astype(own.dtype),
            from_partner(as_sent(own_pair), "ctx", level),
            own_pair,
        )
        partners.append(other_pair)
        if level + 1 < levels:
            own_pair = merge_level(own_pair, other_pair, bit_list[level])
    key_set = jnp.concatenate(
        [to_heads(key_rows, heads)] + [to_heads(pair[0], heads) for pair in partners], axis=2
    )
    value_set = jnp.concatenate(
        [to_heads(value_rows, heads)] + [to_heads(pair[1], heads) for pair in partners], axis=2
    )
    query_four = to_heads(queries, heads)
    grad_four = to_heads(out_grad, heads)
    query_part, key_part, value_part, slope_part = attend(
        query_four, key_set, value_set, grad_four, level_slope, block
    )
    slope_grad = lax.psum(slope_part, ("dp", "ctx"))
    head = width // heads
    grad_keys = jnp.zeros((seqs, heads, block, head), jnp.float32)
    grad_values = jnp.zeros((seqs, heads, block, head), jnp.float32)
    for level in reversed(range(levels)):
        own_keys, sent_keys = split_level(grad_keys, key_part, bit_list[level], level, block)
        own_values, sent_values = split_level(
            grad_values, value_part, bit_list[level], level, block
        )
        back_keys, back_values = from_partner((sent_keys, sent_values), "ctx", level)
        grad_keys = own_keys + back_keys.astype(jnp.float32)
        grad_values = own_values + back_values.astype(jnp.float32)
    key_grad = from_heads((grad_keys + key_part[:, :, :block]).astype(jnp.bfloat16))
    value_grad = from_heads((grad_values + value_part[:, :, :block]).astype(jnp.bfloat16))
    return (from_heads(query_part.astype(jnp.bfloat16)), key_grad, value_grad, slope_grad)


def solution(mesh):
    placed = (
        P("dp", "ctx", None),
        P("dp", "ctx", None),
        P("dp", "ctx", None),
        P("dp", "ctx", None),
        P(),
    )
    return jax.shard_map(
        shards,
        mesh=mesh,
        in_specs=placed,
        out_specs=(P("dp", "ctx", None), P("dp", "ctx", None), P("dp", "ctx", None), P()),
        check_vma=False,
    )
```

profile of v0, /device:TPU:1, one launch (start us, length us, event | category | flops | bytes accessed | tf_op | source)
XLA Modules:
  0.0 589.4 jit_solution(14422107451718763266)
XLA Ops:
  0.7 5.0 collective-permute-start
  5.6 1.9 collective-permute-start.6
  7.7 1.6 copy.84
  9.3 1.6 copy.119
  10.9 2.0 fusion.33
  15.2 9.6 %collective-permute-done.6 = bf16[2,64,2048]{2,1,0:T(8,128)(2,1)} collective-permute-done((bf16[2,64,2048]{2,1,0:T(8,128)(2,1)}, bf16[2,64,2048]{2,1,0:T(8,128)(2,1)}, u32[]{:S(2)}, u32[]{:S(2)}) %collective-permute-start.6) | collective-permute-done | bytes 524320 | tf_op jit(solution)/shard_map/ppermute | solution.py:16
  24.8 1.6 copy.116
  26.8 1.6 copy.82
  30.0 9.8 %collective-permute-start.1 = (bf16[2,64,2048]{2,0,1:T(2,128)(2,1)S(1)}, bf16[2,64,2048]{2,0,1:T(2,128)(2,1)S(1)}, u32[]{:S(2)}, u32[]{:S(2)}) collective-permute-start(bf16[2,64,2048]{2,0,1:T(2,128)(2,1)S(1)} %broadcast_select_fusion.9), channel_id=1, source_target_pairs={{0,2},{1,3},{2,0},{3,1},{4,6},{5,7},{6,4},{7,5},{8,10},{9,11},{10,... | collective-permute-start | bytes 1572872 | tf_op jit(solution)/shard_map/ppermute | solution.py:16
  41.5 1.9 collective-permute-start.7
  44.0 2.0 fusion.32
  46.0 2.0 fusion.29
  48.0 25.8 %collective-permute-done.1 = bf16[2,64,2048]{2,0,1:T(2,128)(2,1)S(1)} collective-permute-done((bf16[2,64,2048]{2,0,1:T(2,128)(2,1)S(1)}, bf16[2,64,2048]{2,0,1:T(2,128)(2,1)S(1)}, u32[]{:S(2)}, u32[]{:S(2)}) %collective-permute-start.1) | collective-permute-done | bytes 524320 | tf_op jit(solution)/shard_map/ppermute | solution.py:16
  76.5 8.4 %collective-permute-start.2 = (bf16[2,64,2048]{2,0,1:T(2,128)(2,1)S(1)}, bf16[2,64,2048]{2,0,1:T(2,128)(2,1)S(1)}, u32[]{:S(2)}, u32[]{:S(2)}) collective-permute-start(bf16[2,64,2048]{2,0,1:T(2,128)(2,1)S(1)} %broadcast_select_fusion.7), channel_id=1, source_target_pairs={{0,4},{1,5},{2,6},{3,7},{4,0},{5,1},{6,2},{7,3},{8,12},{9,13},{10,... | collective-permute-start | bytes 1572872 | tf_op jit(solution)/shard_map/ppermute | solution.py:16
  87.3 1.9 broadcast_select_fusion.6
  89.3 30.1 %collective-permute-start.8 = (bf16[2,64,2048]{2,0,1:T(2,128)(2,1)}, bf16[2,64,2048]{2,0,1:T(2,128)(2,1)S(1)}, u32[]{:S(2)}, u32[]{:S(2)}) collective-permute-start(bf16[2,64,2048]{2,0,1:T(2,128)(2,1)} %broadcast_select_fusion.6), channel_id=1, source_target_pairs={{0,4},{1,5},{2,6},{3,7},{4,0},{5,1},{6,2},{7,3},{8,12},{9,13},{10,... | collective-permute-start | bytes 1572872 | tf_op jit(solution)/shard_map/ppermute | solution.py:16
  120.5 2.1 bitcast_dynamic-update-slice_fusion.9
  123.9 1.6 convert.39
  128.0 3.2 collective-permute-start.3
  132.2 9.6 %collective-permute-done.8 = bf16[2,64,2048]{2,0,1:T(2,128)(2,1)S(1)} collective-permute-done((bf16[2,64,2048]{2,0,1:T(2,128)(2,1)}, bf16[2,64,2048]{2,0,1:T(2,128)(2,1)S(1)}, u32[]{:S(2)}, u32[]{:S(2)}) %collective-permute-start.8) | collective-permute-done | bytes 524320 | tf_op jit(solution)/shard_map/ppermute | solution.py:16
  142.8 1.9 broadcast_select_fusion.4
  144.7 3.6 collective-permute-start.9
  149.4 2.1 bitcast_dynamic-update-slice_fusion.8
  152.9 1.6 convert.41
  157.1 4.2 collective-permute-start.4
  163.2 1.9 broadcast_select_fusion.2
  165.2 2.0 collective-permute-start.10
  168.3 2.1 bitcast_dynamic-update-slice_fusion.7
  171.7 1.6 convert.43
  173.7 22.1 %collective-permute-done.4 = bf16[2,64,2048]{2,0,1:T(2,128)(2,1)S(1)} collective-permute-done((bf16[2,64,2048]{2,0,1:T(2,128)(2,1)S(1)}, bf16[2,64,2048]{2,0,1:T(2,128)(2,1)S(1)}, u32[]{:S(2)}, u32[]{:S(2)}) %collective-permute-start.4) | collective-permute-done | bytes 524320 | tf_op jit(solution)/shard_map/ppermute | solution.py:16
  196.8 1.9 broadcast_select_fusion.1
  198.8 6.3 %collective-permute-start.5 = (bf16[2,64,2048]{2,0,1:T(2,128)(2,1)}, bf16[2,64,2048]{2,0,1:T(2,128)(2,1)S(1)}, u32[]{:S(2)}, u32[]{:S(2)}) collective-permute-start(bf16[2,64,2048]{2,0,1:T(2,128)(2,1)} %broadcast_select_fusion.1), channel_id=1, source_target_pairs={{0,32},{1,33},{2,34},{3,35},{4,36},{5,37},{6,38},{7,39},{8,40},{9,... | collective-permute-start | bytes 1572872 | tf_op jit(solution)/shard_map/ppermute | solution.py:16
  205.0 2.2 collective-permute-done.10
  208.1 1.9 broadcast_select_fusion
  210.1 20.2 %collective-permute-start.11 = (bf16[2,64,2048]{2,0,1:T(2,128)(2,1)}, bf16[2,64,2048]{2,0,1:T(2,128)(2,1)S(1)}, u32[]{:S(2)}, u32[]{:S(2)}) collective-permute-start(bf16[2,64,2048]{2,0,1:T(2,128)(2,1)} %broadcast_select_fusion), channel_id=1, source_target_pairs={{0,32},{1,33},{2,34},{3,35},{4,36},{5,37},{6,38},{7,39},{8,40},{9,... | collective-permute-start | bytes 1572872 | tf_op jit(solution)/shard_map/ppermute | solution.py:16
  234.4 22.0 %collective-permute-done.11 = bf16[2,64,2048]{2,0,1:T(2,128)(2,1)S(1)} collective-permute-done((bf16[2,64,2048]{2,0,1:T(2,128)(2,1)}, bf16[2,64,2048]{2,0,1:T(2,128)(2,1)S(1)}, u32[]{:S(2)}, u32[]{:S(2)}) %collective-permute-start.11) | collective-permute-done | bytes 524320 | tf_op jit(solution)/shard_map/ppermute | solution.py:16
  257.7 3.7 fusion.31
  261.4 1.6 fusion.123
  263.0 1.9 fusion.28
  266.1 2.1 multiply_reduce_fusion
  269.1 5.7 collective-permute-start.18
  275.7 101.6 %psum.7 = f32[16]{0:T(128)} all-reduce(f32[16]{0:T(128)S(1)} %get-tuple-element.26), channel_id=1, replica_groups=mesh['dp'=8,'ctx'=64] {'dp','ctx'}, use_global_device_ids=true, to_apply=%region_4.5 | all-reduce | flops 16 | bytes 128 | tf_op jit(solution)/shard_map/psum | solution.py:133
  379.5 5.8 collective-permute-start.12
  387.2 1.9 collective-permute-start.19
  389.1 20.6 %collective-permute-done.12 = bf16[2,16,64,128]{3,2,1,0:T(8,128)(2,1)S(1)} collective-permute-done((bf16[2,16,64,128]{3,2,1,0:T(8,128)(2,1)S(1)}, bf16[2,16,64,128]{3,2,1,0:T(8,128)(2,1)S(1)}, u32[]{:S(2)}, u32[]{:S(2)}) %collective-permute-start.12) | collective-permute-done | bytes 524320 | tf_op jit(solution)/shard_map/ppermute | solution.py:16
  410.5 1.9 collective-permute-start.13
  412.4 30.1 %collective-permute-done.19 = bf16[2,16,64,128]{3,2,1,0:T(8,128)(2,1)S(1)} collective-permute-done((bf16[2,16,64,128]{3,2,1,0:T(8,128)(2,1)S(1)}, bf16[2,16,64,128]{3,2,1,0:T(8,128)(2,1)S(1)}, u32[]{:S(2)}, u32[]{:S(2)}) %collective-permute-start.19) | collective-permute-done | bytes 524320 | tf_op jit(solution)/shard_map/ppermute | solution.py:16
  443.8 2.4 collective-permute-start.20
  446.3 7.6 %collective-permute-done.13 = bf16[2,16,64,128]{3,2,1,0:T(8,128)(2,1)S(1)} collective-permute-done((bf16[2,16,64,128]{3,2,1,0:T(8,128)(2,1)S(1)}, bf16[2,16,64,128]{3,2,1,0:T(8,128)(2,1)S(1)}, u32[]{:S(2)}, u32[]{:S(2)}) %collective-permute-start.13) | collective-permute-done | bytes 524320 | tf_op jit(solution)/shard_map/ppermute | solution.py:16
  455.0 2.4 collective-permute-start.14
  457.5 7.5 %collective-permute-done.20 = bf16[2,16,64,128]{3,2,1,0:T(8,128)(2,1)S(1)} collective-permute-done((bf16[2,16,64,128]{3,2,1,0:T(8,128)(2,1)S(1)}, bf16[2,16,64,128]{3,2,1,0:T(8,128)(2,1)S(1)}, u32[]{:S(2)}, u32[]{:S(2)}) %collective-permute-start.20) | collective-permute-done | bytes 524320 | tf_op jit(solution)/shard_map/ppermute | solution.py:16
  466.3 5.2 collective-permute-start.21
  471.5 4.7 collective-permute-done.14
  477.5 5.2 collective-permute-start.15
  482.7 24.9 %collective-permute-done.21 = bf16[2,16,64,128]{3,2,1,0:T(8,128)(2,1)S(1)} collective-permute-done((bf16[2,16,64,128]{3,2,1,0:T(8,128)(2,1)S(1)}, bf16[2,16,64,128]{3,2,1,0:T(8,128)(2,1)S(1)}, u32[]{:S(2)}, u32[]{:S(2)}) %collective-permute-start.21) | collective-permute-done | bytes 524320 | tf_op jit(solution)/shard_map/ppermute | solution.py:16
  508.9 1.9 collective-permute-start.22
  510.8 8.1 %collective-permute-done.15 = bf16[2,16,64,128]{3,2,1,0:T(8,128)(2,1)S(1)} collective-permute-done((bf16[2,16,64,128]{3,2,1,0:T(8,128)(2,1)S(1)}, bf16[2,16,64,128]{3,2,1,0:T(8,128)(2,1)S(1)}, u32[]{:S(2)}, u32[]{:S(2)}) %collective-permute-start.15) | collective-permute-done | bytes 524320 | tf_op jit(solution)/shard_map/ppermute | solution.py:16
  520.2 2.2 collective-permute-start.16
  522.4 31.5 %collective-permute-done.22 = bf16[2,16,64,128]{3,2,1,0:T(8,128)(2,1)S(1)} collective-permute-done((bf16[2,16,64,128]{3,2,1,0:T(8,128)(2,1)S(1)}, bf16[2,16,64,128]{3,2,1,0:T(8,128)(2,1)S(1)}, u32[]{:S(2)}, u32[]{:S(2)}) %collective-permute-start.22) | collective-permute-done | bytes 524320 | tf_op jit(solution)/shard_map/ppermute | solution.py:16
  555.1 1.9 collective-permute-start.23
  557.0 8.1 %collective-permute-done.16 = bf16[2,16,64,128]{3,2,1,0:T(8,128)(2,1)S(1)} collective-permute-done((bf16[2,16,64,128]{3,2,1,0:T(8,128)(2,1)S(1)}, bf16[2,16,64,128]{3,2,1,0:T(8,128)(2,1)S(1)}, u32[]{:S(2)}, u32[]{:S(2)}) %collective-permute-start.16) | collective-permute-done | bytes 524320 | tf_op jit(solution)/shard_map/ppermute | solution.py:16
  566.4 1.9 collective-permute-start.17
  568.3 8.0 %collective-permute-done.23 = bf16[2,16,64,128]{3,2,1,0:T(8,128)(2,1)S(1)} collective-permute-done((bf16[2,16,64,128]{3,2,1,0:T(8,128)(2,1)S(1)}, bf16[2,16,64,128]{3,2,1,0:T(8,128)(2,1)S(1)}, u32[]{:S(2)}, u32[]{:S(2)}) %collective-permute-start.23) | collective-permute-done | bytes 524320 | tf_op jit(solution)/shard_map/ppermute | solution.py:16
  577.7 9.9 %collective-permute-done.17 = bf16[2,16,64,128]{3,2,1,0:T(8,128)(2,1)S(1)} collective-permute-done((bf16[2,16,64,128]{3,2,1,0:T(8,128)(2,1)S(1)}, bf16[2,16,64,128]{3,2,1,0:T(8,128)(2,1)S(1)}, u32[]{:S(2)}, u32[]{:S(2)}) %collective-permute-start.17) | collective-permute-done | bytes 524320 | tf_op jit(solution)/shard_map/ppermute | solution.py:16
  (145 shorter events, 55.8 us)
Async XLA Ops:
  0.6 262.4 %copy-start = (bf16[2,64,2048]{2,1,0:T(8,128)(2,1)S(1)}, bf16[2,64,2048]{2,1,0:T(8,128)(2,1)}, u32[]{:S(2)}) copy-start(bf16[2,64,2048]{2,1,0:T(8,128)(2,1)} %param.8) | copy-start | bytes 1572868
  0.6 12.2 %copy-start.5 = (bf16[2,64,2048]{2,1,0:T(8,128)(2,1)S(1)}, bf16[2,64,2048]{2,1,0:T(8,128)(2,1)}, u32[]{:S(2)}) copy-start(bf16[2,64,2048]{2,1,0:T(8,128)(2,1)} %param.7) | copy-start | bytes 1572868
  0.7 26.2 %collective-permute-start = (bf16[2,64,2048]{2,1,0:T(8,128)(2,1)}, bf16[2,64,2048]{2,1,0:T(8,128)(2,1)}, u32[]{:S(2)}, u32[]{:S(2)}) collective-permute-start(bf16[2,64,2048]{2,1,0:T(8,128)(2,1)} %param.6), channel_id=1, source_target_pairs={{0,1},{1,0},{2,3},{3,2},{4,5},{5,4},{6,7},{7,6},{8,9},{9,8},{10,11... | collective-permute-start | bytes 1572872 | tf_op jit(solution)/shard_map/ppermute | solution.py:16
  5.6 19.1 %collective-permute-start.6 = (bf16[2,64,2048]{2,1,0:T(8,128)(2,1)}, bf16[2,64,2048]{2,1,0:T(8,128)(2,1)}, u32[]{:S(2)}, u32[]{:S(2)}) collective-permute-start(bf16[2,64,2048]{2,1,0:T(8,128)(2,1)} %param.7), channel_id=1, source_target_pairs={{0,1},{1,0},{2,3},{3,2},{4,5},{5,4},{6,7},{7,6},{8,9},{9,8},{10,11... | collective-permute-start | bytes 1572872 | tf_op jit(solution)/shard_map/ppermute | solution.py:16
  7.7 7.0 %copy-start.7 = (f32[16]{0:T(128)S(1)}, f32[16]{0:T(128)}, u32[]{:S(2)}) copy-start(f32[16]{0:T(128)} %param.9) | copy-start | bytes 196
  30.0 43.8 %collective-permute-start.1 = (bf16[2,64,2048]{2,0,1:T(2,128)(2,1)S(1)}, bf16[2,64,2048]{2,0,1:T(2,128)(2,1)S(1)}, u32[]{:S(2)}, u32[]{:S(2)}) collective-permute-start(bf16[2,64,2048]{2,0,1:T(2,128)(2,1)S(1)} %broadcast_select_fusion.9), channel_id=1, source_target_pairs={{0,2},{1,3},{2,0},{3,1},{4,6},{5,7},{6,4},{7,5},{8,10},{9,11},{10,... | collective-permute-start | bytes 1572872 | tf_op jit(solution)/shard_map/ppermute | solution.py:16
  41.5 44.3 %collective-permute-start.7 = (bf16[2,64,2048]{2,0,1:T(2,128)(2,1)S(1)}, bf16[2,64,2048]{2,0,1:T(2,128)(2,1)S(1)}, u32[]{:S(2)}, u32[]{:S(2)}) collective-permute-start(bf16[2,64,2048]{2,0,1:T(2,128)(2,1)S(1)} %broadcast_select_fusion.8), channel_id=1, source_target_pairs={{0,2},{1,3},{2,0},{3,1},{4,6},{5,7},{6,4},{7,5},{8,10},{9,11},{10,... | collective-permute-start | bytes 1572872 | tf_op jit(solution)/shard_map/ppermute | solution.py:16
  76.5 49.4 %collective-permute-start.2 = (bf16[2,64,2048]{2,0,1:T(2,128)(2,1)S(1)}, bf16[2,64,2048]{2,0,1:T(2,128)(2,1)S(1)}, u32[]{:S(2)}, u32[]{:S(2)}) collective-permute-start(bf16[2,64,2048]{2,0,1:T(2,128)(2,1)S(1)} %broadcast_select_fusion.7), channel_id=1, source_target_pairs={{0,4},{1,5},{2,6},{3,7},{4,0},{5,1},{6,2},{7,3},{8,12},{9,13},{10,... | collective-permute-start | bytes 1572872 | tf_op jit(solution)/shard_map/ppermute | solution.py:16
  89.3 52.5 %collective-permute-start.8 = (bf16[2,64,2048]{2,0,1:T(2,128)(2,1)}, bf16[2,64,2048]{2,0,1:T(2,128)(2,1)S(1)}, u32[]{:S(2)}, u32[]{:S(2)}) collective-permute-start(bf16[2,64,2048]{2,0,1:T(2,128)(2,1)} %broadcast_select_fusion.6), channel_id=1, source_target_pairs={{0,4},{1,5},{2,6},{3,7},{4,0},{5,1},{6,2},{7,3},{8,12},{9,13},{10,... | collective-permute-start | bytes 1572872 | tf_op jit(solution)/shard_map/ppermute | solution.py:16
  128.0 26.9 %collective-permute-start.3 = (bf16[2,64,2048]{2,0,1:T(2,128)(2,1)S(1)}, bf16[2,64,2048]{2,0,1:T(2,128)(2,1)S(1)}, u32[]{:S(2)}, u32[]{:S(2)}) collective-permute-start(bf16[2,64,2048]{2,0,1:T(2,128)(2,1)S(1)} %broadcast_select_fusion.5), channel_id=1, source_target_pairs={{0,8},{1,9},{2,10},{3,11},{4,12},{5,13},{6,14},{7,15},{8,0},{9,1},... | collective-permute-start | bytes 1572872 | tf_op jit(solution)/shard_map/ppermute | solution.py:16
  144.7 17.5 %collective-permute-start.9 = (bf16[2,64,2048]{2,0,1:T(2,128)(2,1)}, bf16[2,64,2048]{2,0,1:T(2,128)(2,1)S(1)}, u32[]{:S(2)}, u32[]{:S(2)}) collective-permute-start(bf16[2,64,2048]{2,0,1:T(2,128)(2,1)} %broadcast_select_fusion.4), channel_id=1, source_target_pairs={{0,8},{1,9},{2,10},{3,11},{4,12},{5,13},{6,14},{7,15},{8,0},{9,1},... | collective-permute-start | bytes 1572872 | tf_op jit(solution)/shard_map/ppermute | solution.py:16
  157.1 38.8 %collective-permute-start.4 = (bf16[2,64,2048]{2,0,1:T(2,128)(2,1)S(1)}, bf16[2,64,2048]{2,0,1:T(2,128)(2,1)S(1)}, u32[]{:S(2)}, u32[]{:S(2)}) collective-permute-start(bf16[2,64,2048]{2,0,1:T(2,128)(2,1)S(1)} %broadcast_select_fusion.3), channel_id=1, source_target_pairs={{0,16},{1,17},{2,18},{3,19},{4,20},{5,21},{6,22},{7,23},{8,24},{9,... | collective-permute-start | bytes 1572872 | tf_op jit(solution)/shard_map/ppermute | solution.py:16
  165.2 42.0 %collective-permute-start.10 = (bf16[2,64,2048]{2,0,1:T(2,128)(2,1)}, bf16[2,64,2048]{2,0,1:T(2,128)(2,1)S(1)}, u32[]{:S(2)}, u32[]{:S(2)}) collective-permute-start(bf16[2,64,2048]{2,0,1:T(2,128)(2,1)} %broadcast_select_fusion.2), channel_id=1, source_target_pairs={{0,16},{1,17},{2,18},{3,19},{4,20},{5,21},{6,22},{7,23},{8,24},{9,... | collective-permute-start | bytes 1572872 | tf_op jit(solution)/shard_map/ppermute | solution.py:16
  198.8 34.3 %collective-permute-start.5 = (bf16[2,64,2048]{2,0,1:T(2,128)(2,1)}, bf16[2,64,2048]{2,0,1:T(2,128)(2,1)S(1)}, u32[]{:S(2)}, u32[]{:S(2)}) collective-permute-start(bf16[2,64,2048]{2,0,1:T(2,128)(2,1)} %broadcast_select_fusion.1), channel_id=1, source_target_pairs={{0,32},{1,33},{2,34},{3,35},{4,36},{5,37},{6,38},{7,39},{8,40},{9,... | collective-permute-start | bytes 1572872 | tf_op jit(solution)/shard_map/ppermute | solution.py:16
  210.1 46.3 %collective-permute-start.11 = (bf16[2,64,2048]{2,0,1:T(2,128)(2,1)}, bf16[2,64,2048]{2,0,1:T(2,128)(2,1)S(1)}, u32[]{:S(2)}, u32[]{:S(2)}) collective-permute-start(bf16[2,64,2048]{2,0,1:T(2,128)(2,1)} %broadcast_select_fusion), channel_id=1, source_target_pairs={{0,32},{1,33},{2,34},{3,35},{4,36},{5,37},{6,38},{7,39},{8,40},{9,... | collective-permute-start | bytes 1572872 | tf_op jit(solution)/shard_map/ppermute | solution.py:16
  230.6 27.1 %copy-start.4 = (bf16[2,64,2048]{2,1,0:T(8,128)(2,1)S(1)}, bf16[2,64,2048]{2,1,0:T(8,128)(2,1)}, u32[]{:S(2)}) copy-start(bf16[2,64,2048]{2,1,0:T(8,128)(2,1)} %param.5) | copy-start | bytes 1572868
  263.0 2.0 copy-start.6
  265.1 3.2 copy-start.3
  266.1 8.7 %copy-start.2 = (bf16[2,16,448,128]{3,2,1,0:T(8,128)(2,1)S(1)}, bf16[2,16,448,128]{3,2,1,0:T(8,128)(2,1)}, u32[]{:S(2)}) copy-start(bf16[2,16,448,128]{3,2,1,0:T(8,128)(2,1)} %bitcast_dynamic-update-slice_fusion.5) | copy-start | bytes 11010052
  269.1 116.2 %collective-permute-start.18 = (bf16[2,16,64,128]{3,2,1,0:T(8,128)(2,1)}, bf16[2,16,64,128]{3,2,1,0:T(8,128)(2,1)}, u32[]{:S(2)}, u32[]{:S(2)}) collective-permute-start(bf16[2,16,64,128]{3,2,1,0:T(8,128)(2,1)} %slice.726), channel_id=1, source_target_pairs={{0,32},{1,33},{2,34},{3,35},{4,36},{5,37},{6,38},{7,39},{8,40},{9,... | collective-permute-start | bytes 1572872 | tf_op jit(solution)/shard_map/ppermute | solution.py:16
  377.3 9.7 %slice-start = ((s8[7340032]{0:T(1024)(128)(4,1)}), s8[4194304]{0:T(1024)(128)(4,1)S(1)}, s32[]{:S(2)}) async-start(s8[7340032]{0:T(1024)(128)(4,1)} %bitcast.564), calls=%async_computation | async-start | bytes 8388608
  378.2 8.7 %slice-start.1 = ((s8[7340032]{0:T(1024)(128)(4,1)}), s8[3145728]{0:T(1024)(128)(4,1)S(1)}, s32[]{:S(2)}) async-start(s8[7340032]{0:T(1024)(128)(4,1)} %bitcast.564), calls=%async_computation.1 | async-start | bytes 6291456
  379.5 30.2 %collective-permute-start.12 = (bf16[2,16,64,128]{3,2,1,0:T(8,128)(2,1)S(1)}, bf16[2,16,64,128]{3,2,1,0:T(8,128)(2,1)S(1)}, u32[]{:S(2)}, u32[]{:S(2)}) collective-permute-start(bf16[2,16,64,128]{3,2,1,0:T(8,128)(2,1)S(1)} %slice.727), channel_id=1, source_target_pairs={{0,32},{1,33},{2,34},{3,35},{4,36},{5,37},{6,38},{7,39},{8,40},{9,... | collective-permute-start | bytes 1572872 | tf_op jit(solution)/shard_map/ppermute | solution.py:16
  387.2 55.4 %collective-permute-start.19 = (bf16[2,16,64,128]{3,2,1,0:T(8,128)(2,1)S(1)}, bf16[2,16,64,128]{3,2,1,0:T(8,128)(2,1)S(1)}, u32[]{:S(2)}, u32[]{:S(2)}) collective-permute-start(bf16[2,16,64,128]{3,2,1,0:T(8,128)(2,1)S(1)} %fusion.17), channel_id=1, source_target_pairs={{0,16},{1,17},{2,18},{3,19},{4,20},{5,21},{6,22},{7,23},{8,24},{9,... | collective-permute-start | bytes 1572872 | tf_op jit(solution)/shard_map/ppermute | solution.py:16
  410.5 43.3 %collective-permute-start.13 = (bf16[2,16,64,128]{3,2,1,0:T(8,128)(2,1)S(1)}, bf16[2,16,64,128]{3,2,1,0:T(8,128)(2,1)S(1)}, u32[]{:S(2)}, u32[]{:S(2)}) collective-permute-start(bf16[2,16,64,128]{3,2,1,0:T(8,128)(2,1)S(1)} %fusion.23), channel_id=1, source_target_pairs={{0,16},{1,17},{2,18},{3,19},{4,20},{5,21},{6,22},{7,23},{8,24},{9,... | collective-permute-start | bytes 1572872 | tf_op jit(solution)/shard_map/ppermute | solution.py:16
  443.8 21.2 %collective-permute-start.20 = (bf16[2,16,64,128]{3,2,1,0:T(8,128)(2,1)S(1)}, bf16[2,16,64,128]{3,2,1,0:T(8,128)(2,1)S(1)}, u32[]{:S(2)}, u32[]{:S(2)}) collective-permute-start(bf16[2,16,64,128]{3,2,1,0:T(8,128)(2,1)S(1)} %fusion.16), channel_id=1, source_target_pairs={{0,8},{1,9},{2,10},{3,11},{4,12},{5,13},{6,14},{7,15},{8,0},{9,1},... | collective-permute-start | bytes 1572872 | tf_op jit(solution)/shard_map/ppermute | solution.py:16
  455.0 21.2 %collective-permute-start.14 = (bf16[2,16,64,128]{3,2,1,0:T(8,128)(2,1)S(1)}, bf16[2,16,64,128]{3,2,1,0:T(8,128)(2,1)S(1)}, u32[]{:S(2)}, u32[]{:S(2)}) collective-permute-start(bf16[2,16,64,128]{3,2,1,0:T(8,128)(2,1)S(1)} %fusion.22), channel_id=1, source_target_pairs={{0,8},{1,9},{2,10},{3,11},{4,12},{5,13},{6,14},{7,15},{8,0},{9,1},... | collective-permute-start | bytes 1572872 | tf_op jit(solution)/shard_map/ppermute | solution.py:16
  466.3 41.4 %collective-permute-start.21 = (bf16[2,16,64,128]{3,2,1,0:T(8,128)(2,1)S(1)}, bf16[2,16,64,128]{3,2,1,0:T(8,128)(2,1)S(1)}, u32[]{:S(2)}, u32[]{:S(2)}) collective-permute-start(bf16[2,16,64,128]{3,2,1,0:T(8,128)(2,1)S(1)} %fusion.15), channel_id=1, source_target_pairs={{0,4},{1,5},{2,6},{3,7},{4,0},{5,1},{6,2},{7,3},{8,12},{9,13},{10,... | collective-permute-start | bytes 1572872 | tf_op jit(solution)/shard_map/ppermute | solution.py:16
  477.5 41.5 %collective-permute-start.15 = (bf16[2,16,64,128]{3,2,1,0:T(8,128)(2,1)S(1)}, bf16[2,16,64,128]{3,2,1,0:T(8,128)(2,1)S(1)}, u32[]{:S(2)}, u32[]{:S(2)}) collective-permute-start(bf16[2,16,64,128]{3,2,1,0:T(8,128)(2,1)S(1)} %fusion.21), channel_id=1, source_target_pairs={{0,4},{1,5},{2,6},{3,7},{4,0},{5,1},{6,2},{7,3},{8,12},{9,13},{10,... | collective-permute-start | bytes 1572872 | tf_op jit(solution)/shard_map/ppermute | solution.py:16
  508.9 45.0 %collective-permute-start.22 = (bf16[2,16,64,128]{3,2,1,0:T(8,128)(2,1)S(1)}, bf16[2,16,64,128]{3,2,1,0:T(8,128)(2,1)S(1)}, u32[]{:S(2)}, u32[]{:S(2)}) collective-permute-start(bf16[2,16,64,128]{3,2,1,0:T(8,128)(2,1)S(1)} %fusion.14), channel_id=1, source_target_pairs={{0,2},{1,3},{2,0},{3,1},{4,6},{5,7},{6,4},{7,5},{8,10},{9,11},{10,... | collective-permute-start | bytes 1572872 | tf_op jit(solution)/shard_map/ppermute | solution.py:16
  520.2 44.9 %collective-permute-start.16 = (bf16[2,16,64,128]{3,2,1,0:T(8,128)(2,1)S(1)}, bf16[2,16,64,128]{3,2,1,0:T(8,128)(2,1)S(1)}, u32[]{:S(2)}, u32[]{:S(2)}) collective-permute-start(bf16[2,16,64,128]{3,2,1,0:T(8,128)(2,1)S(1)} %fusion.20), channel_id=1, source_target_pairs={{0,2},{1,3},{2,0},{3,1},{4,6},{5,7},{6,4},{7,5},{8,10},{9,11},{10,... | collective-permute-start | bytes 1572872 | tf_op jit(solution)/shard_map/ppermute | solution.py:16
  555.1 21.2 %collective-permute-start.23 = (bf16[2,16,64,128]{3,2,1,0:T(8,128)(2,1)S(1)}, bf16[2,16,64,128]{3,2,1,0:T(8,128)(2,1)S(1)}, u32[]{:S(2)}, u32[]{:S(2)}) collective-permute-start(bf16[2,16,64,128]{3,2,1,0:T(8,128)(2,1)S(1)} %fusion.13), channel_id=1, source_target_pairs={{0,1},{1,0},{2,3},{3,2},{4,5},{5,4},{6,7},{7,6},{8,9},{9,8},{10,11... | collective-permute-start | bytes 1572872 | tf_op jit(solution)/shard_map/ppermute | solution.py:16
  566.4 21.2 %collective-permute-start.17 = (bf16[2,16,64,128]{3,2,1,0:T(8,128)(2,1)S(1)}, bf16[2,16,64,128]{3,2,1,0:T(8,128)(2,1)S(1)}, u32[]{:S(2)}, u32[]{:S(2)}) collective-permute-start(bf16[2,16,64,128]{3,2,1,0:T(8,128)(2,1)S(1)} %fusion.19), channel_id=1, source_target_pairs={{0,1},{1,0},{2,3},{3,2},{4,5},{5,4},{6,7},{7,6},{8,9},{9,8},{10,11... | collective-permute-start | bytes 1572872 | tf_op jit(solution)/shard_map/ppermute | solution.py:16
  576.7 12.2 %copy-start.1 = (bf16[2,64,2048]{2,1,0:T(8,128)(2,1)S(1)}, bf16[2,64,2048]{2,1,0:T(8,128)(2,1)}, u32[]{:S(2)}) copy-start(bf16[2,64,2048]{2,1,0:T(8,128)(2,1)} %param.8) | copy-start | bytes 1572868
where the time goes:
time: 599 us; the launch traced here: 589 us
  waiting for transfers between devices  252 us (42%)
  starting transfers between devices  135 us (23%)
  blocking collectives  102 us (17%)
  other arithmetic  45 us (8%)
  local copies, waits for them, and re-layouts  42.2 us (7%)
  matrix products  10.8 us (2%)
    ppermute x24, waiting for transfers between devices, from_partner(): return lax.ppermute(value, axis, pairs)  252 us
    ppermute x24, starting transfers between devices, from_partner(): return lax.ppermute(value, axis, pairs)  135 us
    psum x1, blocking collectives, shards(): slope_grad = lax.psum(slope_part, ('dp', 'ctx'))  102 us
    unnamed x32, local copies, waits for them, and re-layouts  18.5 us
    select_n x10, other arithmetic, merge_level(): jnp.where(flag == 1, jnp.concatenate([other_small, own_small], axis=1), j...  15.5 us
  transfers between devices with their start and end apart: 24, of which 17 were waited for; matrix products, arithmetic and copies ran while one was open for 14% of the time, Pallas kernels for 0%

commit v1 on v0

v1 whole, which is shorter than its diff:
```python
import functools
import math

import jax
import jax.numpy as jnp
from jax import lax
from jax.experimental import pallas as pl
from jax.experimental.pallas import tpu as pltpu
from jax.sharding import PartitionSpec as P

MESH = pl.DeviceIdType.MESH
F32 = jnp.float32
BF16 = jnp.bfloat16
N = 8
BLOCK = 64
WIDE = 256
HEAD = 128
PAIR = 2 * BLOCK
UPPER = 3 * BLOCK
KEYS = PAIR + 2 * BLOCK + UPPER
LOCAL = 4 * BLOCK + 2 * BLOCK
LOG2E = math.log2(math.e)


def ring(step):
    def one(index, carry):
        half = index // 2
        step(half + 1 + (index % 2) * (N - 2 - 2 * half))
        return carry

    lax.fori_loop(0, N - 1, one, 0)


def halving(rows, columns):
    row = lax.broadcasted_iota(jnp.int32, (rows, columns), 0)
    column = lax.broadcasted_iota(jnp.int32, (rows, columns), 1)
    return jnp.where(column // 2 == row, 0.5, 0.0).astype(BF16)


def dot(left, right, dims=((1,), (0,))):
    return lax.dot_general(left, right, (dims, ((), ())), preferred_element_type=F32)


def spread_local(rows):
    token = lax.broadcasted_iota(jnp.int32, (rows, LOCAL), 0)
    cell = lax.broadcasted_iota(jnp.int32, (rows, LOCAL), 1)
    first = cell < 4 * BLOCK
    have = jnp.where(first, token // 2, token // 4 + 4 * BLOCK)
    return jnp.where(have == cell, jnp.where(first, 0.5, 0.25), 0.0).astype(BF16)


def spread_upper(rows):
    token = lax.broadcasted_iota(jnp.int32, (rows, UPPER), 0)
    cell = lax.broadcasted_iota(jnp.int32, (rows, UPPER), 1)
    three = cell < BLOCK
    four = cell < 2 * BLOCK
    want = jnp.where(three, cell, jnp.where(four, cell % 32, cell % 16))
    have = jnp.where(three, token // 8, jnp.where(four, token // 16, token // 32))
    size = jnp.where(three, 0.125, jnp.where(four, 0.0625, 0.03125))
    return jnp.where(want == have, size, 0.0).astype(BF16)


def kernel(
    slope_ref, k_in, v_in, q_in, g_in,
    dq_out, dk_out, dv_out, slope_out,
    xb, l1, l2, y3, y4, y5, yb, spread1, spread2,
    token_acc, quad_acc, upper_acc, c_local, y_back, c_upper, ob,
    slope_acc, slope_z, slope_mid, slope_y, slope_top, slope_dp,
    own_sem, in_send, in_recv, y_send, y_recv, back_send, back_recv,
    out_own, out_send, out_recv, s_send, s_recv,
):
    dp = lax.axis_index("dp")
    ctx = lax.axis_index("ctx")
    z = ctx % N
    y = ctx // N
    ins = (k_in, v_in, q_in, g_in)
    outs = (dq_out, dk_out, dv_out)

    def at_z(d):
        return (z + d) % N

    def on_z(d):
        return (dp, y * N + at_z(d))

    def on_y(row):
        return (dp, row * N + z)

    def on_dp(d):
        return ((dp + d) % N, ctx)

    def columns(place):
        return pl.ds(pl.multiple_of(place * WIDE, WIDE), WIDE)

    def remote(src, dst, send, recv, device):
        return pltpu.make_async_remote_copy(
            src_ref=src, dst_ref=dst, send_sem=send, recv_sem=recv,
            device_id=device, device_id_type=MESH,
        )

    barrier = pltpu.get_barrier_semaphore()
    @ring
    def _(d):
        for device in (on_z(d), on_y((y + d) % N), on_dp(d)):
            pl.semaphore_signal(barrier, inc=1, device_id=device, device_id_type=MESH)

    pl.semaphore_wait(barrier, 3 * (N - 1))

    def own_copy(a):
        return pltpu.make_async_copy(ins[a].at[:, :, columns(z)], xb.at[a, :, z], own_sem.at[a])

    def in_copy(a, d):
        return remote(
            ins[a].at[:, :, columns(at_z(d))], xb.at[a, :, z],
            in_send.at[a, d], in_recv.at[a, d], on_z(d),
        )

    def in_arrival(a, d):
        return remote(
            ins[a].at[:, :, columns(at_z(d))], xb.at[a, :, (z + N - d) % N],
            in_send.at[a, d], in_recv.at[a, d], on_z(d),
        )

    for group in ((0, 1), (2, 3)):
        ring(lambda d, group=group: [in_copy(a, d).start() for a in group])
        for a in group:
            own_copy(a).start()

    spread1[...] = spread_local(N * BLOCK)
    spread2[...] = spread_upper(N * BLOCK)
    quad_acc[...] = jnp.zeros_like(quad_acc)
    upper_acc[...] = jnp.zeros_like(upper_acc)
    slope_acc[...] = jnp.zeros_like(slope_acc)

    for a in (0, 1):
        own_copy(a).wait()
        ring(lambda d, a=a: in_arrival(a, d).wait_recv())

    pool = halving(BLOCK, PAIR)
    pool4 = halving(32, 64)
    pool5 = halving(16, 32)

    def summarize(kv, s):
        for p in range(4):
            cells = xb[kv, s, 2 * p : 2 * p + 2].reshape(PAIR, WIDE)
            l1[kv, s, p] = dot(pool, cells).astype(BF16)
        for r in range(2):
            cells = l1[kv, s, 2 * r : 2 * r + 2].reshape(PAIR, WIDE)
            l2[kv, s, r] = dot(pool, cells).astype(BF16)
        third = dot(pool, l2[kv, s].reshape(PAIR, WIDE)).astype(BF16)
        fourth = dot(pool4, third).astype(BF16)
        y3[kv, s] = third
        y4[kv, s] = fourth
        y5[kv, s] = dot(pool5, fourth).astype(BF16)

    for kv in range(2):
        for s in range(2):
            summarize(kv, s)

    row3 = y + 1 - 2 * (y % 2)
    base4 = 2 * (y // 2 + 1 - 2 * ((y // 2) % 2))
    base5 = 4 * (1 - y // 4)

    def rows(start, size):
        return pl.ds(pl.multiple_of(start, size), size)

    def y_copies(recv_index_of_self):
        copies = [
            remote(y3, yb.at[:, :, pl.ds(0, 64)], y_send.at[0], y_recv.at[0], on_y(row3))
        ]
        for j in range(2):
            slot = y % 2 if recv_index_of_self else j
            copies.append(
                remote(
                    y4, yb.at[:, :, rows(64 + 32 * slot, 32)],
                    y_send.at[1 + j], y_recv.at[1 + slot], on_y(base4 + j),
                )
            )
        for j in range(4):
            slot = y % 4 if recv_index_of_self else j
            copies.append(
                remote(
                    y5, yb.at[:, :, rows(128 + 16 * slot, 16)],
                    y_send.at[3 + j], y_recv.at[3 + slot], on_y(base5 + j),
                )
            )
        return copies

    def back_copies(recv_index_of_self):
        copies = [
            remote(
                y_back.at[:, :, pl.ds(0, 64)], c_upper.at[:, :, pl.ds(0, 64)],
                back_send.at[0], back_recv.at[0], on_y(row3),
            )
        ]
        for j in range(2):
            slot = y % 2 if recv_index_of_self else j
            copies.append(
                remote(
                    y_back.at[:, :, pl.ds(64 + 32 * j, 32)],
                    c_upper.at[:, :, rows(64 + 32 * slot, 32)],
                    back_send.at[1 + j], back_recv.at[1 + slot], on_y(base4 + j),
                )
            )
        for j in range(4):
            slot = y % 4 if recv_index_of_self else j
            copies.append(
                remote(
                    y_back.at[:, :, pl.ds(128 + 16 * j, 16)],
                    c_upper.at[:, :, rows(128 + 16 * slot, 16)],
                    back_send.at[3 + j], back_recv.at[3 + slot], on_y(base5 + j),
                )
            )
        return copies

    for copy in y_copies(True):
        copy.start()
    for a in (2, 3):
        own_copy(a).wait()
        ring(lambda d, a=a: in_arrival(a, d).wait_recv())
    for copy in y_copies(False):
        copy.wait_recv()

    scale = 1.0 / math.sqrt(HEAD)
    groups = ((0, PAIR, 0),) + tuple(
        (PAIR + BLOCK * (level - 1), PAIR + BLOCK * level, level) for level in range(1, 6)
    )

    def attend(p, s):
        sibling = p + 1 - 2 * (p % 2)
        quad = 1 - p // 2
        sets = []
        for kv in range(2):
            sets.append(
                jnp.concatenate(
                    [
                        xb[kv, s, pl.ds(2 * p, 2)].reshape(PAIR, WIDE),
                        l1[kv, s, sibling],
                        l2[kv, s, quad],
                        yb[kv, s],
                    ],
                    axis=0,
                )
            )
        query_rows = xb[2, s, pl.ds(2 * p, 2)].reshape(PAIR, WIDE)
        grad_rows = xb[3, s, pl.ds(2 * p, 2)].reshape(PAIR, WIDE)
        for h in range(2):
            lanes = slice(h * HEAD, (h + 1) * HEAD)
            slope = slope_ref[2 * z + h]
            keys, values = sets[0][:, lanes], sets[1][:, lanes]
            query, grad = query_rows[:, lanes], grad_rows[:, lanes]
            raw = dot(keys, query, ((1,), (1,)))
            up = dot(values, grad, ((1,), (1,)))
            scores = []
            top = None
            for first, last, level in groups:
                part = raw[first:last] * (scale * LOG2E)
                if level:
                    part = part + (slope * (LOG2E * level) + float(level))
                scores.append(part)
                best = jnp.max(part, axis=0, keepdims=True)
                top = best if top is None else jnp.maximum(top, best)
            weights = [jnp.exp2(part - top) for part in scores]
            total = sum(jnp.sum(part, axis=0, keepdims=True) for part in weights)
            inverse = 1.0 / total
            probs = [part * inverse for part in weights]
            probs_low = [part.astype(BF16) for part in probs]
            ups = [up[first:last] for first, last, _ in groups]
            delta = sum(
                jnp.sum(low.astype(F32) * part, axis=0, keepdims=True)
                for low, part in zip(probs_low, ups)
            )
            ds = [prob * (part - delta) for prob, part in zip(probs, ups)]
            tilted = sum(
                float(level) * jnp.sum(part.reshape(BLOCK // 8, 8, HEAD), axis=0)
                for part, (_, _, level) in zip(ds, groups)
                if level
            )
            slope_acc[h] += tilted
            ds_low = jnp.concatenate([part.astype(BF16) for part in ds], axis=0)
            p_low = jnp.concatenate(probs_low, axis=0)
            query_part = dot(ds_low, keys, ((0,), (0,))) * scale
            ob[0, s, pl.ds(2 * p, 2), :, lanes] = query_part.astype(BF16).reshape(2, BLOCK, HEAD)
            for kv, part in ((0, dot(ds_low, query)), (1, dot(p_low, grad))):
                token_acc[kv, s, p, :, lanes] = part[:PAIR]
                c_local[kv, s, pl.ds(sibling * BLOCK, BLOCK), lanes] = part[
                    PAIR : PAIR + BLOCK
                ].astype(BF16)
                quad_acc[kv, s, quad, :, lanes] += part[PAIR + BLOCK : PAIR + 2 * BLOCK]
                upper_acc[kv, s, :, lanes] += part[PAIR + 2 * BLOCK :]

    for p in range(4):
        for s in range(2):
            attend(p, s)

    def out_copy(o, d):
        return remote(
            ob.at[o, :, at_z(d)], outs[o].at[:, :, columns(z)],
            out_send.at[o, d], out_recv.at[o, d], on_z(d),
        )

    def out_arrival(o, d):
        return remote(
            ob.at[o, :, at_z(d)], outs[o].at[:, :, columns((z + N - d) % N)],
            out_send.at[o, d], out_recv.at[o, d], on_z(d),
        )

    def out_copy_own(o):
        return pltpu.make_async_copy(ob.at[o, :, z], outs[o].at[:, :, columns(z)], out_own.at[o])

    def slope_copy(phase, src, dst, place, d, device):
        return remote(src, dst.at[place], s_send.at[phase, d], s_recv.at[phase, d], device)

    ring(lambda d: slope_copy(0, slope_acc, slope_z, z, d, on_z(d)).start())

    y_back[...] = upper_acc[...].astype(BF16)
    for copy in back_copies(True):
        copy.start()
    ring(lambda d: out_copy(0, d).start())
    out_copy_own(0).start()
    for kv in range(2):
        for s in range(2):
            for r in range(2):
                c_local[kv, s, 256 + 64 * r : 320 + 64 * r] = quad_acc[kv, s, r].astype(BF16)

    slope_z[z] = slope_acc[...]
    ring(lambda d: slope_copy(0, slope_acc, slope_z, (z + N - d) % N, d, on_z(d)).wait_recv())
    slope_mid[...] = jnp.sum(slope_z[...], axis=2).reshape(2 * N, HEAD)
    ring(lambda d: slope_copy(1, slope_mid, slope_y, y, d, on_y((y + d) % N)).start())

    for copy in back_copies(False):
        copy.wait_recv()
    for kv in (0, 1):
        for s in range(2):
            total = token_acc[kv, s].reshape(N * BLOCK, WIDE)
            total = total + dot(spread1[...], c_local[kv, s]) + dot(spread2[...], c_upper[kv, s])
            if kv == 0:
                total = total * scale
            ob[1 + kv, s] = total.astype(BF16).reshape(N, BLOCK, WIDE)
        ring(lambda d, kv=kv: out_copy(1 + kv, d).start())
        out_copy_own(1 + kv).start()

    slope_y[y] = slope_mid[...]
    ring(lambda d: slope_copy(1, slope_mid, slope_y, (y + N - d) % N, d, on_y((y + d) % N)).wait_recv())
    slope_top[...] = sum(slope_y[i] for i in range(N))
    ring(lambda d: slope_copy(2, slope_top, slope_dp, dp, d, on_dp(d)).start())
    slope_dp[dp] = slope_top[...]
    ring(lambda d: slope_copy(2, slope_top, slope_dp, (dp + N - d) % N, d, on_dp(d)).wait_recv())
    everything = sum(slope_dp[i] for i in range(N))
    slope_out[...] = jnp.broadcast_to(
        jnp.sum(everything, axis=1, keepdims=True), (2 * N, HEAD)
    )

    for o in range(3):
        out_copy_own(o).wait()
        ring(lambda d, o=o: out_arrival(o, d).wait_recv())
    for a in range(4):
        ring(lambda d, a=a: in_copy(a, d).wait_send())
    for copy in y_copies(True) + back_copies(True):
        copy.wait_send()
    for o in range(3):
        ring(lambda d, o=o: out_copy(o, d).wait_send())

    @ring
    def _(d):
        slope_copy(0, slope_acc, slope_z, z, d, on_z(d)).wait_send()
        slope_copy(1, slope_mid, slope_y, y, d, on_y((y + d) % N)).wait_send()
        slope_copy(2, slope_top, slope_dp, dp, d, on_dp(d)).wait_send()


def shards(queries, key_rows, value_rows, out_grad, level_slope):
    seqs = queries.shape[0]
    whole = jax.ShapeDtypeStruct(queries.shape, BF16)
    any_spec = pl.BlockSpec(memory_space=pl.ANY)
    dma = pltpu.SemaphoreType.DMA
    vmem = pltpu.VMEM
    query_grad, key_grad, value_grad, slopes = pl.pallas_call(
        kernel,
        out_shape=(whole, whole, whole, jax.ShapeDtypeStruct((2 * N, HEAD), F32)),
        in_specs=[pl.BlockSpec(memory_space=pltpu.SMEM)] + [any_spec] * 4,
        out_specs=(any_spec, any_spec, any_spec, pl.BlockSpec(memory_space=pltpu.VMEM)),
        scratch_shapes=[
            vmem((4, seqs, N, BLOCK, WIDE), BF16),
            vmem((2, seqs, 4, BLOCK, WIDE), BF16),
            vmem((2, seqs, 2, BLOCK, WIDE), BF16),
            vmem((2, seqs, 64, WIDE), BF16),
            vmem((2, seqs, 32, WIDE), BF16),
            vmem((2, seqs, 16, WIDE), BF16),
            vmem((2, seqs, UPPER, WIDE), BF16),
            vmem((N * BLOCK, LOCAL), BF16),
            vmem((N * BLOCK, UPPER), BF16),
            vmem((2, seqs, 4, PAIR, WIDE), F32),
            vmem((2, seqs, 2, BLOCK, WIDE), F32),
            vmem((2, seqs, UPPER, WIDE), F32),
            vmem((2, seqs, LOCAL, WIDE), BF16),
            vmem((2, seqs, UPPER, WIDE), BF16),
            vmem((2, seqs, UPPER, WIDE), BF16),
            vmem((3, seqs, N, BLOCK, WIDE), BF16),
            vmem((2, 8, HEAD), F32),
            vmem((N, 2, 8, HEAD), F32),
            vmem((2 * N, HEAD), F32),
            vmem((N, 2 * N, HEAD), F32),
            vmem((2 * N, HEAD), F32),
            vmem((N, 2 * N, HEAD), F32),
            dma((4,)),
            dma((4, N)),
            dma((4, N)),
            dma((7,)),
            dma((7,)),
            dma((7,)),
            dma((7,)),
            dma((3,)),
            dma((3, N)),
            dma((3, N)),
            dma((3, N)),
            dma((3, N)),
        ],
        compiler_params=pltpu.CompilerParams(
            collective_id=0, has_side_effects=True, vmem_limit_bytes=48 * 1024 * 1024
        ),
        name="hierarchical_attention",
    )(level_slope, key_rows, value_rows, queries, out_grad)
    return query_grad, key_grad, value_grad, slopes[:, 0]


def solution(mesh):
    placed = (P("dp", "ctx", None),) * 4 + (P(),)
    return jax.shard_map(
        shards,
        mesh=mesh,
        in_specs=placed,
        out_specs=(P("dp", "ctx", None),) * 3 + (P(),),
        check_vma=False,
    )
```

time: 599 us -> 117 us (0.20); the launches traced: 589 us -> 115 us
  waiting for transfers between devices: 252 us -> 0 us
  starting transfers between devices: 135 us -> 0 us
  Pallas kernels: 0 us -> 106 us
  blocking collectives: 102 us -> 0 us
  other arithmetic: 45 us -> 0 us
  local copies, waits for them, and re-layouts: 42.2 us -> 7.82 us
  matrix products: 10.8 us -> 0 us
    ppermute x24 -> x0, waiting for transfers between devices: 252 us -> none  [from_partner(): return lax.ppermute(value, axis, pairs)]
    ppermute x24 -> x0, starting transfers between devices: 135 us -> none  [from_partner(): return lax.ppermute(value, axis, pairs)]
    pallas_call x0 -> x1, Pallas kernels: none -> 106 us  [shards(): pl.pallas_call(kernel, out_shape=(whole, whole, whole, jax.ShapeDtypeStru...]
    psum x1 -> x0, blocking collectives: 102 us -> none  [shards(): slope_grad = lax.psum(slope_part, ('dp', 'ctx'))]
    convert_element_type x47 -> x0, other arithmetic: 23.2 us -> none  [the longest x16 11.3 us: pair_mean(): cells.reshape(cells.shape[:-2] + (cells.shape[-2] // 2, 2, cells.shape[-1]))]
    select_n x11 -> x0, other arithmetic: 15.5 us -> none  [the longest x10 15.5 us: merge_level(): jnp.where(flag == 1, jnp.concatenate([other_small, own_small], axis=1), j...]
    unnamed x32 -> x13, local copies, waits for them, and re-layouts: 18.5 us -> 7.19 us
    dot_general x6 -> x0, matrix products: 10.8 us -> none  [product(): return jnp.einsum(form, left, right, preferred_element_type=jnp.float32)]
  transfers between devices with their start and end apart: 24 -> 0, of which waited for: 17 -> 0; matrix products, arithmetic and copies ran while one was open for 14% -> 0% of each run, Pallas kernels for 0% -> 0%
where the time goes in v1:
time: 117 us; the launch traced here: 115 us
  Pallas kernels  106 us (91%)
  local copies, waits for them, and re-layouts  7.82 us (7%)
    pallas_call x1, Pallas kernels, shards(): pl.pallas_call(kernel, out_shape=(whole, whole, whole, jax.ShapeDtypeStru...  106 us
    unnamed x13, local copies, waits for them, and re-layouts  7.19 us

profile of v1, /device:TPU:1, one launch (start us, length us, event | category | flops | bytes accessed | tf_op | source)
XLA Modules:
  0.0 114.8 jit_solution(1521273394397063562)
XLA Ops:
  0.6 0.0 copy-start
  0.6 1.0 copy-done
  1.7 0.0 copy-start.1
  1.7 1.0 copy-done.1
  2.7 0.0 copy-start.2
  2.7 1.0 copy-done.2
  3.8 0.0 copy-start.3
  3.8 1.0 copy-done.3
  4.8 0.0 copy-start.4
  4.8 0.7 copy-done.4
  5.5 106.4 %hierarchical_attention.1 = (bf16[2,64,2048]{2,1,0:T(8,128)(2,1)S(1)}, bf16[2,64,2048]{2,1,0:T(8,128)(2,1)S(1)}, bf16[2,64,2048]{2,1,0:T(8,128)(2,1)S(1)}, f32[16,128]{1,0:T(8,128)S(1)}) custom-call(f32[16]{0:T(128)S(1)} %copy-done.4, bf16[2,64,2048]{2,1,0:T(8,128)(2,1)S(1)} %copy-done, bf16[2,64,2048]{2,1,0:T(8,128)(2,1)S(1)} %copy-done.1, ...), custom_call_target="tpu_custom_call" | custom-call | tf_op jit(solution)/shard_map/hierarchical_attention/pallas_call | solution.py:376
  111.8 0.6 slice_reduce_fusion
  112.5 0.8 copy.12
  113.2 0.8 copy.13
  114.0 0.8 copy.14
Async XLA Ops:
  0.6 1.0 copy-start
  1.7 1.0 copy-start.1
  2.7 1.0 copy-start.2
  3.8 1.0 copy-start.3
  4.8 0.7 copy-start.4

commit v2 on v1

--- a/solution.py
+++ b/solution.py
@@ -24,11 +24,10 @@
 
 def ring(step):
     def one(index, carry):
-        half = index // 2
-        step(half + 1 + (index % 2) * (N - 2 - 2 * half))
+        step(index)
         return carry
 
-    lax.fori_loop(0, N - 1, one, 0)
+    lax.fori_loop(1, N, one, 0)
 
 
 def halving(rows, columns):
@@ -65,7 +64,7 @@
     dq_out, dk_out, dv_out, slope_out,
     xb, l1, l2, y3, y4, y5, yb, spread1, spread2,
     token_acc, quad_acc, upper_acc, c_local, y_back, c_upper, ob,
-    slope_acc, slope_z, slope_mid, slope_y, slope_top, slope_dp,
+    slope_acc, slope_y, slope_mid, slope_dp, slope_top, slope_z,
     own_sem, in_send, in_recv, y_send, y_recv, back_send, back_recv,
     out_own, out_send, out_recv, s_send, s_recv,
 ):
@@ -76,11 +75,14 @@
     ins = (k_in, v_in, q_in, g_in)
     outs = (dq_out, dk_out, dv_out)
 
-    def at_z(d):
-        return (z + d) % N
-
-    def on_z(d):
-        return (dp, y * N + at_z(d))
+    def at_z(e):
+        place = z
+        for bit in (1, 2, 4):
+            place = place + (1 - 2 * ((z // bit) % 2)) * ((e // bit) % 2) * bit
+        return place
+
+    def on_z(e):
+        return (dp, y * N + at_z(e))
 
     def on_y(row):
         return (dp, row * N + z)
@@ -106,19 +108,20 @@
     pl.semaphore_wait(barrier, 3 * (N - 1))
 
     def own_copy(a):
-        return pltpu.make_async_copy(ins[a].at[:, :, columns(z)], xb.at[a, :, z], own_sem.at[a])
+        return pltpu.make_async_copy(ins[a].at[:, :, columns(z)], xb.at[a, :, 0], own_sem.at[a])
 
     def in_copy(a, d):
         return remote(
-            ins[a].at[:, :, columns(at_z(d))], xb.at[a, :, z],
+            ins[a].at[:, :, columns(at_z(d))], xb.at[a, :, d],
             in_send.at[a, d], in_recv.at[a, d], on_z(d),
         )
 
-    def in_arrival(a, d):
-        return remote(
-            ins[a].at[:, :, columns(at_z(d))], xb.at[a, :, (z + N - d) % N],
-            in_send.at[a, d], in_recv.at[a, d], on_z(d),
-        )
+    def arrive(a, p):
+        if p == 0:
+            own_copy(a).wait()
+        else:
+            in_copy(a, 2 * p).wait_recv()
+        in_copy(a, 2 * p + 1).wait_recv()
 
     for group in ((0, 1), (2, 3)):
         ring(lambda d, group=group: [in_copy(a, d).start() for a in group])
@@ -131,30 +134,25 @@
     upper_acc[...] = jnp.zeros_like(upper_acc)
     slope_acc[...] = jnp.zeros_like(slope_acc)
 
-    for a in (0, 1):
-        own_copy(a).wait()
-        ring(lambda d, a=a: in_arrival(a, d).wait_recv())
-
     pool = halving(BLOCK, PAIR)
     pool4 = halving(32, 64)
     pool5 = halving(16, 32)
 
-    def summarize(kv, s):
-        for p in range(4):
-            cells = xb[kv, s, 2 * p : 2 * p + 2].reshape(PAIR, WIDE)
-            l1[kv, s, p] = dot(pool, cells).astype(BF16)
-        for r in range(2):
-            cells = l1[kv, s, 2 * r : 2 * r + 2].reshape(PAIR, WIDE)
-            l2[kv, s, r] = dot(pool, cells).astype(BF16)
-        third = dot(pool, l2[kv, s].reshape(PAIR, WIDE)).astype(BF16)
-        fourth = dot(pool4, third).astype(BF16)
-        y3[kv, s] = third
-        y4[kv, s] = fourth
-        y5[kv, s] = dot(pool5, fourth).astype(BF16)
-
-    for kv in range(2):
-        for s in range(2):
-            summarize(kv, s)
+    for p in range(4):
+        for kv in range(2):
+            arrive(kv, p)
+            for s in range(2):
+                cells = xb[kv, s, 2 * p : 2 * p + 2].reshape(PAIR, WIDE)
+                l1[kv, s, p] = dot(pool, cells).astype(BF16)
+                if p % 2:
+                    cells = l1[kv, s, p - 1 : p + 1].reshape(PAIR, WIDE)
+                    l2[kv, s, p // 2] = dot(pool, cells).astype(BF16)
+                if p == 3:
+                    third = dot(pool, l2[kv, s].reshape(PAIR, WIDE)).astype(BF16)
+                    fourth = dot(pool4, third).astype(BF16)
+                    y3[kv, s] = third
+                    y4[kv, s] = fourth
+                    y5[kv, s] = dot(pool5, fourth).astype(BF16)
 
     row3 = y + 1 - 2 * (y % 2)
     base4 = 2 * (y // 2 + 1 - 2 * ((y // 2) % 2))
@@ -214,11 +212,23 @@
 
     for copy in y_copies(True):
         copy.start()
-    for a in (2, 3):
-        own_copy(a).wait()
-        ring(lambda d, a=a: in_arrival(a, d).wait_recv())
     for copy in y_copies(False):
         copy.wait_recv()
+
+    def out_copy(o, d):
+        return remote(
+            ob.at[o, :, d], outs[o].at[:, :, columns(z)],
+            out_send.at[o, d], out_recv.at[o, d], on_z(d),
+        )
+
+    def out_arrival(o, d):
+        return remote(
+            ob.at[o, :, d], outs[o].at[:, :, columns(at_z(d))],
+            out_send.at[o, d], out_recv.at[o, d], on_z(d),
+        )
+
+    def out_copy_own(o):
+        return pltpu.make_async_copy(ob.at[o, :, 0], outs[o].at[:, :, columns(z)], out_own.at[o])
 
     scale = 1.0 / math.sqrt(HEAD)
     groups = ((0, PAIR, 0),) + tuple(
@@ -289,44 +299,37 @@
                 upper_acc[kv, s, :, lanes] += part[PAIR + 2 * BLOCK :]
 
     for p in range(4):
+        for a in (2, 3):
+            arrive(a, p)
         for s in range(2):
             attend(p, s)
-
-    def out_copy(o, d):
-        return remote(
-            ob.at[o, :, at_z(d)], outs[o].at[:, :, columns(z)],
-            out_send.at[o, d], out_recv.at[o, d], on_z(d),
-        )
-
-    def out_arrival(o, d):
-        return remote(
-            ob.at[o, :, at_z(d)], outs[o].at[:, :, columns((z + N - d) % N)],
-            out_send.at[o, d], out_recv.at[o, d], on_z(d),
-        )
-
-    def out_copy_own(o):
-        return pltpu.make_async_copy(ob.at[o, :, z], outs[o].at[:, :, columns(z)], out_own.at[o])
+        if p == 0:
+            out_copy_own(0).start()
+        else:
+            out_copy(0, 2 * p).start()
+        out_copy(0, 2 * p + 1).start()
 
     def slope_copy(phase, src, dst, place, d, device):
         return remote(src, dst.at[place], s_send.at[phase, d], s_recv.at[phase, d], device)
 
-    ring(lambda d: slope_copy(0, slope_acc, slope_z, z, d, on_z(d)).start())
+    def slope_y_copy(d, place):
+        return slope_copy(0, slope_acc, slope_y, place, d, on_y((y + d) % N))
+
+    def slope_dp_copy(d, place):
+        return slope_copy(1, slope_mid, slope_dp, place, d, on_dp(d))
+
+    def slope_z_copy(d, place):
+        return slope_copy(2, slope_top, slope_z, place, d, on_z(d))
 
     y_back[...] = upper_acc[...].astype(BF16)
     for copy in back_copies(True):
         copy.start()
-    ring(lambda d: out_copy(0, d).start())
-    out_copy_own(0).start()
+    ring(lambda d: slope_y_copy(d, y).start())
+    slope_y[y] = slope_acc[...]
     for kv in range(2):
         for s in range(2):
             for r in range(2):
                 c_local[kv, s, 256 + 64 * r : 320 + 64 * r] = quad_acc[kv, s, r].astype(BF16)
-
-    slope_z[z] = slope_acc[...]
-    ring(lambda d: slope_copy(0, slope_acc, slope_z, (z + N - d) % N, d, on_z(d)).wait_recv())
-    slope_mid[...] = jnp.sum(slope_z[...], axis=2).reshape(2 * N, HEAD)
-    ring(lambda d: slope_copy(1, slope_mid, slope_y, y, d, on_y((y + d) % N)).start())
-
     for copy in back_copies(False):
         copy.wait_recv()
     for kv in (0, 1):
@@ -336,19 +339,22 @@
             if kv == 0:
                 total = total * scale
             ob[1 + kv, s] = total.astype(BF16).reshape(N, BLOCK, WIDE)
+        if kv == 1:
+            ring(lambda d: slope_dp_copy(d, (dp + N - d) % N).wait_recv())
+            slope_top[...] = sum(slope_dp[i] for i in range(N))
+            ring(lambda d: slope_z_copy(d, z).start())
+            slope_z[z] = slope_top[...]
         ring(lambda d, kv=kv: out_copy(1 + kv, d).start())
         out_copy_own(1 + kv).start()
-
-    slope_y[y] = slope_mid[...]
-    ring(lambda d: slope_copy(1, slope_mid, slope_y, (y + N - d) % N, d, on_y((y + d) % N)).wait_recv())
-    slope_top[...] = sum(slope_y[i] for i in range(N))
-    ring(lambda d: slope_copy(2, slope_top, slope_dp, dp, d, on_dp(d)).start())
-    slope_dp[dp] = slope_top[...]
-    ring(lambda d: slope_copy(2, slope_top, slope_dp, (dp + N - d) % N, d, on_dp(d)).wait_recv())
-    everything = sum(slope_dp[i] for i in range(N))
-    slope_out[...] = jnp.broadcast_to(
-        jnp.sum(everything, axis=1, keepdims=True), (2 * N, HEAD)
-    )
+        if kv == 0:
+            ring(lambda d: slope_y_copy(d, (y + N - d) % N).wait_recv())
+            slope_mid[...] = sum(slope_y[i] for i in range(N))
+            ring(lambda d: slope_dp_copy(d, dp).start())
+            slope_dp[dp] = slope_mid[...]
+    ring(lambda d: slope_z_copy(d, at_z(d)).wait_recv())
+    for owner in range(N):
+        for h in range(2):
+            slope_out[2 * owner + h] = jnp.sum(slope_z[owner, h])
 
     for o in range(3):
         out_copy_own(o).wait()
@@ -360,24 +366,22 @@
     for o in range(3):
         ring(lambda d, o=o: out_copy(o, d).wait_send())
 
-    @ring
-    def _(d):
-        slope_copy(0, slope_acc, slope_z, z, d, on_z(d)).wait_send()
-        slope_copy(1, slope_mid, slope_y, y, d, on_y((y + d) % N)).wait_send()
-        slope_copy(2, slope_top, slope_dp, dp, d, on_dp(d)).wait_send()
+    ring(lambda d: slope_y_copy(d, y).wait_send())
+    ring(lambda d: slope_dp_copy(d, dp).wait_send())
+    ring(lambda d: slope_z_copy(d, z).wait_send())
 
 
 def shards(queries, key_rows, value_rows, out_grad, level_slope):
     seqs = queries.shape[0]
     whole = jax.ShapeDtypeStruct(queries.shape, BF16)
-    any_spec = pl.BlockSpec(memory_space=pl.ANY)
+    any_spec = pl.BlockSpec(memory_space=pltpu.HBM)
     dma = pltpu.SemaphoreType.DMA
     vmem = pltpu.VMEM
     query_grad, key_grad, value_grad, slopes = pl.pallas_call(
         kernel,
-        out_shape=(whole, whole, whole, jax.ShapeDtypeStruct((2 * N, HEAD), F32)),
+        out_shape=(whole, whole, whole, jax.ShapeDtypeStruct((2 * N,), F32)),
         in_specs=[pl.BlockSpec(memory_space=pltpu.SMEM)] + [any_spec] * 4,
-        out_specs=(any_spec, any_spec, any_spec, pl.BlockSpec(memory_space=pltpu.VMEM)),
+        out_specs=(any_spec, any_spec, any_spec, pl.BlockSpec(memory_space=pltpu.SMEM)),
         scratch_shapes=[
             vmem((4, seqs, N, BLOCK, WIDE), BF16),
             vmem((2, seqs, 4, BLOCK, WIDE), BF16),
@@ -397,10 +401,10 @@
             vmem((3, seqs, N, BLOCK, WIDE), BF16),
             vmem((2, 8, HEAD), F32),
             vmem((N, 2, 8, HEAD), F32),
-            vmem((2 * N, HEAD), F32),
-            vmem((N, 2 * N, HEAD), F32),
-            vmem((2 * N, HEAD), F32),
-            vmem((N, 2 * N, HEAD), F32),
+            vmem((2, 8, HEAD), F32),
+            vmem((N, 2, 8, HEAD), F32),
+            vmem((2, 8, HEAD), F32),
+            vmem((N, 2, 8, HEAD), F32),
             dma((4,)),
             dma((4, N)),
             dma((4, N)),
@@ -415,11 +419,11 @@
             dma((3, N)),
         ],
         compiler_params=pltpu.CompilerParams(
-            collective_id=0, has_side_effects=True, vmem_limit_bytes=48 * 1024 * 1024
+            collective_id=0, has_side_effects=True, vmem_limit_bytes=67043328
         ),
         name="hierarchical_attention",
     )(level_slope, key_rows, value_rows, queries, out_grad)
-    return query_grad, key_grad, value_grad, slopes[:, 0]
+    return query_grad, key_grad, value_grad, slopes
 
 
 def solution(mesh):

time: 117 us -> 113 us (0.966); the launches traced: 115 us -> 113 us
  local copies, waits for them, and re-layouts: 7.82 us -> 4.48 us
  Pallas kernels: 106 us -> 108 us
    unnamed x13 -> x10, local copies, waits for them, and re-layouts: 7.19 us -> 4.48 us
where the time goes in v2:
time: 113 us
  Pallas kernels  108 us (96%)
  local copies, waits for them, and re-layouts  4.48 us (4%)
    pallas_call x1, Pallas kernels, shards(): pl.pallas_call(kernel, out_shape=(whole, whole, whole, jax.ShapeDtypeStru...  108 us
    unnamed x10, local copies, waits for them, and re-layouts  4.48 us

profile of v2, /device:TPU:1, one launch (start us, length us, event | category | flops | bytes accessed | tf_op | source)
XLA Modules:
  0.0 112.6 jit_solution(18408594939049242572)
XLA Ops:
  0.6 107.5 %hierarchical_attention.1 = (bf16[2,64,2048]{2,1,0:T(8,128)(2,1)}, bf16[2,64,2048]{2,1,0:T(8,128)(2,1)}, bf16[2,64,2048]{2,1,0:T(8,128)(2,1)}, f32[16]{0:T(128)}) custom-call(f32[16]{0:T(128)} %slope_ref.1, bf16[2,64,2048]{2,1,0:T(8,128)(2,1)} %k_in.1, bf16[2,64,2048]{2,1,0:T(8,128)(2,1)} %v_in.1, bf16[2,64,2048]{2,1,0:T(8,128)(2,1)} %q_in.1, ...), custom_call_target="tpu_custom_call" | custom-call | tf_op jit(solution)/shard_map/hierarchical_attention/pallas_call | solution.py:380
  108.2 0.0 copy-start.1
  108.2 1.9 %copy.13 = bf16[2,64,2048]{2,1,0:T(8,128)(2,1)} copy(bf16[2,64,2048]{2,1,0:T(8,128)(2,1)} %get-tuple-element.8) | data formatting | bytes 1048576
  110.1 0.0 copy-done.1
  110.1 0.0 copy-start
  110.1 0.8 copy.14
  110.9 0.4 copy-done
  111.3 0.0 copy-start.2
  111.3 0.8 copy.15
  112.1 0.0 copy-done.2
  112.1 0.5 copy.16
Async XLA Ops:
  108.2 2.0 %copy-start.1 = (bf16[2,64,2048]{2,1,0:T(8,128)(2,1)S(1)}, bf16[2,64,2048]{2,1,0:T(8,128)(2,1)}, u32[]{:S(2)}) copy-start(bf16[2,64,2048]{2,1,0:T(8,128)(2,1)} %get-tuple-element.9) | copy-start | bytes 1572868
  110.1 1.2 %copy-start = (bf16[2,64,2048]{2,1,0:T(8,128)(2,1)S(1)}, bf16[2,64,2048]{2,1,0:T(8,128)(2,1)}, u32[]{:S(2)}) copy-start(bf16[2,64,2048]{2,1,0:T(8,128)(2,1)} %get-tuple-element.10) | copy-start | bytes 1572868
  111.3 0.8 copy-start.2

commit v3 on v2

--- a/solution.py
+++ b/solution.py
@@ -60,12 +60,12 @@
 
 
 def kernel(
-    slope_ref, k_in, v_in, q_in, g_in,
+    slope_in, k_in, v_in, q_in, g_in,
     dq_out, dk_out, dv_out, slope_out,
     xb, l1, l2, y3, y4, y5, yb, spread1, spread2,
     token_acc, quad_acc, upper_acc, c_local, y_back, c_upper, ob,
     slope_acc, slope_y, slope_mid, slope_dp, slope_top, slope_z,
-    own_sem, in_send, in_recv, y_send, y_recv, back_send, back_recv,
+    slope_ref, slope_sem, own_sem, in_send, in_recv, y_send, y_recv, back_send, back_recv,
     out_own, out_send, out_recv, s_send, s_recv,
 ):
     dp = lax.axis_index("dp")
@@ -81,6 +81,15 @@
             place = place + (1 - 2 * ((z // bit) % 2)) * ((e // bit) % 2) * bit
         return place
 
+    def around(step):
+        def one(index, carry):
+            half = index // 2
+            target = (z + half + 1 + (index % 2) * (N - 2 - 2 * half)) % N
+            step(sum(((target // bit + z // bit) % 2) * bit for bit in (1, 2, 4)))
+            return carry
+
+        lax.fori_loop(0, N - 1, one, 0)
+
     def on_z(e):
         return (dp, y * N + at_z(e))
 
@@ -106,6 +115,9 @@
             pl.semaphore_signal(barrier, inc=1, device_id=device, device_id_type=MESH)
 
     pl.semaphore_wait(barrier, 3 * (N - 1))
+
+    slope_copy_in = pltpu.make_async_copy(slope_in, slope_ref, slope_sem.at[0])
+    slope_copy_in.start()
 
     def own_copy(a):
         return pltpu.make_async_copy(ins[a].at[:, :, columns(z)], xb.at[a, :, 0], own_sem.at[a])
@@ -124,7 +136,7 @@
         in_copy(a, 2 * p + 1).wait_recv()
 
     for group in ((0, 1), (2, 3)):
-        ring(lambda d, group=group: [in_copy(a, d).start() for a in group])
+        around(lambda d, group=group: [in_copy(a, d).start() for a in group])
         for a in group:
             own_copy(a).start()
 
@@ -212,6 +224,7 @@
 
     for copy in y_copies(True):
         copy.start()
+    slope_copy_in.wait()
     for copy in y_copies(False):
         copy.wait_recv()
 
@@ -344,7 +357,7 @@
             slope_top[...] = sum(slope_dp[i] for i in range(N))
             ring(lambda d: slope_z_copy(d, z).start())
             slope_z[z] = slope_top[...]
-        ring(lambda d, kv=kv: out_copy(1 + kv, d).start())
+        around(lambda d, kv=kv: out_copy(1 + kv, d).start())
         out_copy_own(1 + kv).start()
         if kv == 0:
             ring(lambda d: slope_y_copy(d, (y + N - d) % N).wait_recv())
@@ -371,16 +384,26 @@
     ring(lambda d: slope_z_copy(d, z).wait_send())
 
 
+def hand_over(*refs):
+    sem = refs[8]
+    copies = [pltpu.make_async_copy(refs[i], refs[4 + i], sem.at[i]) for i in range(4)]
+    for copy in copies:
+        copy.start()
+    for copy in copies:
+        copy.wait()
+
+
 def shards(queries, key_rows, value_rows, out_grad, level_slope):
     seqs = queries.shape[0]
     whole = jax.ShapeDtypeStruct(queries.shape, BF16)
     any_spec = pl.BlockSpec(memory_space=pltpu.HBM)
     dma = pltpu.SemaphoreType.DMA
+    held = pltpu.with_memory_space_constraint
     vmem = pltpu.VMEM
     query_grad, key_grad, value_grad, slopes = pl.pallas_call(
         kernel,
         out_shape=(whole, whole, whole, jax.ShapeDtypeStruct((2 * N,), F32)),
-        in_specs=[pl.BlockSpec(memory_space=pltpu.SMEM)] + [any_spec] * 4,
+        in_specs=[any_spec] * 5,
         out_specs=(any_spec, any_spec, any_spec, pl.BlockSpec(memory_space=pltpu.SMEM)),
         scratch_shapes=[
             vmem((4, seqs, N, BLOCK, WIDE), BF16),
@@ -405,6 +428,8 @@
             vmem((N, 2, 8, HEAD), F32),
             vmem((2, 8, HEAD), F32),
             vmem((N, 2, 8, HEAD), F32),
+            pltpu.SMEM((2 * N,), F32),
+            dma((1,)),
             dma((4,)),
             dma((4, N)),
             dma((4, N)),
@@ -419,11 +444,19 @@
             dma((3, N)),
         ],
         compiler_params=pltpu.CompilerParams(
-            collective_id=0, has_side_effects=True, vmem_limit_bytes=67043328
+            collective_id=0, has_side_effects=True, vmem_limit_bytes=48 * 1024 * 1024
         ),
         name="hierarchical_attention",
-    )(level_slope, key_rows, value_rows, queries, out_grad)
-    return query_grad, key_grad, value_grad, slopes
+    )(*(held(a, pltpu.HBM) for a in (level_slope, key_rows, value_rows, queries, out_grad)))
+    return pl.pallas_call(
+        hand_over,
+        out_shape=(whole, whole, whole, jax.ShapeDtypeStruct((2 * N,), F32)),
+        in_specs=[pl.BlockSpec(memory_space=pl.ANY)] * 4,
+        out_specs=(any_spec,) * 4,
+        scratch_shapes=[dma((4,))],
+        compiler_params=pltpu.CompilerParams(vmem_limit_bytes=1024 * 1024),
+        name="hand_over",
+    )(query_grad, key_grad, value_grad, slopes)
 
 
 def solution(mesh):

time: 113 us -> 107 us (0.947); the launches traced: 113 us -> 105 us
  local copies, waits for them, and re-layouts: 4.48 us -> 0 us
  Pallas kernels: 108 us -> 104 us
    pallas_call x1, Pallas kernels: 108 us -> 103 us  [shards(): pl.pallas_call(kernel, out_shape=(whole, whole, whole, jax.ShapeDtypeStru...]
    unnamed x10 -> x0, local copies, waits for them, and re-layouts: 4.48 us -> none
    pallas_call x0 -> x1, Pallas kernels: none -> 1.18 us  [shards(): pl.pallas_call(hand_over, out_shape=(whole, whole, whole, jax.ShapeDtypeS...]
where the time goes in v3:
time: 107 us; the launch traced here: 105 us
  Pallas kernels  104 us (97%)
    pallas_call x1, Pallas kernels, shards(): pl.pallas_call(kernel, out_shape=(whole, whole, whole, jax.ShapeDtypeStru...  103 us

profile of v3, /device:TPU:1, one launch (start us, length us, event | category | flops | bytes accessed | tf_op | source)
XLA Modules:
  0.0 104.7 jit_solution(11532883456805190320)
XLA Ops:
  0.6 102.9 %hierarchical_attention.1 = (bf16[2,64,2048]{2,1,0:T(8,128)(2,1)S(1)}, bf16[2,64,2048]{2,1,0:T(8,128)(2,1)S(1)}, bf16[2,64,2048]{2,1,0:T(8,128)(2,1)S(1)}, f32[16]{0:T(128)S(1)}) custom-call(f32[16]{0:T(128)} %slope_in.1, bf16[2,64,2048]{2,1,0:T(8,128)(2,1)} %k_in.1, bf16[2,64,2048]{2,1,0:T(8,128)(2,1)} %v_in.1, bf16[2,64,2048]{2,1,0:T(8,128)(2,1)} %q_in.1, ...), custom_call_target="tpu_custom_call" | custom-call | tf_op jit(solution)/shard_map/hierarchical_attention/pallas_call | solution.py:403
  103.5 1.2 %hand_over.1 = (bf16[2,64,2048]{2,1,0:T(8,128)(2,1)}, bf16[2,64,2048]{2,1,0:T(8,128)(2,1)}, bf16[2,64,2048]{2,1,0:T(8,128)(2,1)}, f32[16]{0:T(128)}) custom-call(bf16[2,64,2048]{2,1,0:T(8,128)(2,1)S(1)} %get-tuple-element.8.refs_0_, bf16[2,64,2048]{2,1,0:T(8,128)(2,1)S(1)} %get-tuple-element.9.refs_1_, bf16[2,64,2048]{2,1,0:T(8,128)(2,1)S(1)} %get-tuple-element.10.refs_2_, ...), custom_call_target="tpu_custom_call" | custom-call | tf_op jit(solution)/shard_map/hand_over/pallas_call | solution.py:451

commit v4 on v3

--- a/solution.py
+++ b/solution.py
@@ -20,6 +20,7 @@
 KEYS = PAIR + 2 * BLOCK + UPPER
 LOCAL = 4 * BLOCK + 2 * BLOCK
 LOG2E = math.log2(math.e)
+PAIRS = (0, 1, 3, 2)
 
 
 def ring(step):
@@ -150,16 +151,17 @@
     pool4 = halving(32, 64)
     pool5 = halving(16, 32)
 
-    for p in range(4):
+    for p in PAIRS:
         for kv in range(2):
             arrive(kv, p)
             for s in range(2):
                 cells = xb[kv, s, 2 * p : 2 * p + 2].reshape(PAIR, WIDE)
                 l1[kv, s, p] = dot(pool, cells).astype(BF16)
-                if p % 2:
-                    cells = l1[kv, s, p - 1 : p + 1].reshape(PAIR, WIDE)
-                    l2[kv, s, p // 2] = dot(pool, cells).astype(BF16)
-                if p == 3:
+                if p in (1, 2):
+                    quad = p // 2
+                    cells = l1[kv, s, 2 * quad : 2 * quad + 2].reshape(PAIR, WIDE)
+                    l2[kv, s, quad] = dot(pool, cells).astype(BF16)
+                if p == 2:
                     third = dot(pool, l2[kv, s].reshape(PAIR, WIDE)).astype(BF16)
                     fourth = dot(pool4, third).astype(BF16)
                     y3[kv, s] = third
@@ -222,7 +224,7 @@
             )
         return copies
 
-    for copy in y_copies(True):
+    for copy in reversed(y_copies(True)):
         copy.start()
     slope_copy_in.wait()
     for copy in y_copies(False):
@@ -311,7 +313,7 @@
                 quad_acc[kv, s, quad, :, lanes] += part[PAIR + BLOCK : PAIR + 2 * BLOCK]
                 upper_acc[kv, s, :, lanes] += part[PAIR + 2 * BLOCK :]
 
-    for p in range(4):
+    for p in PAIRS:
         for a in (2, 3):
             arrive(a, p)
         for s in range(2):
@@ -335,7 +337,7 @@
         return slope_copy(2, slope_top, slope_z, place, d, on_z(d))
 
     y_back[...] = upper_acc[...].astype(BF16)
-    for copy in back_copies(True):
+    for copy in reversed(back_copies(True)):
         copy.start()
     ring(lambda d: slope_y_copy(d, y).start())
     slope_y[y] = slope_acc[...]
@@ -343,12 +345,16 @@
         for s in range(2):
             for r in range(2):
                 c_local[kv, s, 256 + 64 * r : 320 + 64 * r] = quad_acc[kv, s, r].astype(BF16)
+    for kv in range(2):
+        for s in range(2):
+            below = dot(spread1[...], c_local[kv, s])
+            token_acc[kv, s] += below.reshape(4, PAIR, WIDE)
     for copy in back_copies(False):
         copy.wait_recv()
     for kv in (0, 1):
         for s in range(2):
             total = token_acc[kv, s].reshape(N * BLOCK, WIDE)
-            total = total + dot(spread1[...], c_local[kv, s]) + dot(spread2[...], c_upper[kv, s])
+            total = total + dot(spread2[...], c_upper[kv, s])
             if kv == 0:
                 total = total * scale
             ob[1 + kv, s] = total.astype(BF16).reshape(N, BLOCK, WIDE)

time: 107 us -> 104 us (0.972)
  the two profiles are of different devices: /device:TPU:1 before, /device:TPU:8 now
where the time goes in v4:
time: 104 us
  Pallas kernels  103 us (99%)
    pallas_call x1, Pallas kernels, shards(): pl.pallas_call(kernel, out_shape=(whole, whole, whole, jax.ShapeDtypeStru...  102 us

profile of v4, /device:TPU:8, one launch (start us, length us, event | category | flops | bytes accessed | tf_op | source)
XLA Modules:
  0.0 103.6 jit_solution(2048022899978535020)
XLA Ops:
  0.6 101.7 %hierarchical_attention.1 = (bf16[2,64,2048]{2,1,0:T(8,128)(2,1)S(1)}, bf16[2,64,2048]{2,1,0:T(8,128)(2,1)S(1)}, bf16[2,64,2048]{2,1,0:T(8,128)(2,1)S(1)}, f32[16]{0:T(128)S(1)}) custom-call(f32[16]{0:T(128)} %slope_in.1, bf16[2,64,2048]{2,1,0:T(8,128)(2,1)} %k_in.1, bf16[2,64,2048]{2,1,0:T(8,128)(2,1)} %v_in.1, bf16[2,64,2048]{2,1,0:T(8,128)(2,1)} %q_in.1, ...), custom_call_target="tpu_custom_call" | custom-call | tf_op jit(solution)/shard_map/hierarchical_attention/pallas_call | solution.py:409
  102.4 1.2 %hand_over.1 = (bf16[2,64,2048]{2,1,0:T(8,128)(2,1)}, bf16[2,64,2048]{2,1,0:T(8,128)(2,1)}, bf16[2,64,2048]{2,1,0:T(8,128)(2,1)}, f32[16]{0:T(128)}) custom-call(bf16[2,64,2048]{2,1,0:T(8,128)(2,1)S(1)} %get-tuple-element.8.refs_0_, bf16[2,64,2048]{2,1,0:T(8,128)(2,1)S(1)} %get-tuple-element.9.refs_1_, bf16[2,64,2048]{2,1,0:T(8,128)(2,1)S(1)} %get-tuple-element.10.refs_2_, ...), custom_call_target="tpu_custom_call" | custom-call | tf_op jit(solution)/shard_map/hand_over/pallas_call | solution.py:457

commit v5 on v4

--- a/solution.py
+++ b/solution.py
@@ -90,6 +90,15 @@
             return carry
 
         lax.fori_loop(0, N - 1, one, 0)
+
+    def inward(step):
+        def one(index, carry):
+            half = index // 2
+            target = (z + half + 1 + (index % 2) * (N - 2 - 2 * half)) % N
+            step(sum(((target // bit + z // bit) % 2) * bit for bit in (1, 2, 4)))
+            return carry
+
+        lax.fori_loop(0, N - 1, lambda i, c: one(N - 2 - i, c), 0)
 
     def on_z(e):
         return (dp, y * N + at_z(e))
@@ -363,7 +372,7 @@
             slope_top[...] = sum(slope_dp[i] for i in range(N))
             ring(lambda d: slope_z_copy(d, z).start())
             slope_z[z] = slope_top[...]
-        around(lambda d, kv=kv: out_copy(1 + kv, d).start())
+        inward(lambda d, kv=kv: out_copy(1 + kv, d).start())
         out_copy_own(1 + kv).start()
         if kv == 0:
             ring(lambda d: slope_y_copy(d, (y + N - d) % N).wait_recv())
@@ -375,24 +384,26 @@
         for h in range(2):
             slope_out[2 * owner + h] = jnp.sum(slope_z[owner, h])
 
-    for o in range(3):
-        out_copy_own(o).wait()
-        ring(lambda d, o=o: out_arrival(o, d).wait_recv())
     for a in range(4):
         ring(lambda d, a=a: in_copy(a, d).wait_send())
     for copy in y_copies(True) + back_copies(True):
         copy.wait_send()
-    for o in range(3):
-        ring(lambda d, o=o: out_copy(o, d).wait_send())
-
     ring(lambda d: slope_y_copy(d, y).wait_send())
     ring(lambda d: slope_dp_copy(d, dp).wait_send())
     ring(lambda d: slope_z_copy(d, z).wait_send())
+    for o in range(3):
+        out_copy_own(o).wait()
+        ring(lambda d, o=o: out_copy(o, d).wait_send())
+    for o in range(3):
+        ring(lambda d, o=o: out_arrival(o, d).wait_recv())
 
 
 def hand_over(*refs):
     sem = refs[8]
-    copies = [pltpu.make_async_copy(refs[i], refs[4 + i], sem.at[i]) for i in range(4)]
+    copies = [pltpu.make_async_copy(refs[3], refs[7], sem.at[6])]
+    for i in range(3):
+        for s in range(2):
+            copies.append(pltpu.make_async_copy(refs[i].at[s], refs[4 + i].at[s], sem.at[2 * i + s]))
     for copy in copies:
         copy.start()
     for copy in copies:
@@ -459,7 +470,7 @@
         out_shape=(whole, whole, whole, jax.ShapeDtypeStruct((2 * N,), F32)),
         in_specs=[pl.BlockSpec(memory_space=pl.ANY)] * 4,
         out_specs=(any_spec,) * 4,
-        scratch_shapes=[dma((4,))],
+        scratch_shapes=[dma((7,))],
         compiler_params=pltpu.CompilerParams(vmem_limit_bytes=1024 * 1024),
         name="hand_over",
     )(query_grad, key_grad, value_grad, slopes)

time: 104 us -> 104 us (level)
  the two profiles are of different devices: /device:TPU:8 before, /device:TPU:1 now
where the time goes in v5:
time: 104 us; the launch traced here: 102 us
  Pallas kernels  102 us (98%)
    pallas_call x1, Pallas kernels, shards(): pl.pallas_call(kernel, out_shape=(whole, whole, whole, jax.ShapeDtypeStru...  100 us

profile of v5, /device:TPU:1, one launch (start us, length us, event | category | flops | bytes accessed | tf_op | source)
XLA Modules:
  0.0 102.3 jit_solution(13246531280138594979)
XLA Ops:
  0.6 100.4 %hierarchical_attention.1 = (bf16[2,64,2048]{2,1,0:T(8,128)(2,1)S(1)}, bf16[2,64,2048]{2,1,0:T(8,128)(2,1)S(1)}, bf16[2,64,2048]{2,1,0:T(8,128)(2,1)S(1)}, f32[16]{0:T(128)S(1)}) custom-call(f32[16]{0:T(128)} %slope_in.1, bf16[2,64,2048]{2,1,0:T(8,128)(2,1)} %k_in.1, bf16[2,64,2048]{2,1,0:T(8,128)(2,1)} %v_in.1, bf16[2,64,2048]{2,1,0:T(8,128)(2,1)} %q_in.1, ...), custom_call_target="tpu_custom_call" | custom-call | tf_op jit(solution)/shard_map/hierarchical_attention/pallas_call | solution.py:420
  101.1 1.2 %hand_over.1 = (bf16[2,64,2048]{2,1,0:T(8,128)(2,1)}, bf16[2,64,2048]{2,1,0:T(8,128)(2,1)}, bf16[2,64,2048]{2,1,0:T(8,128)(2,1)}, f32[16]{0:T(128)}) custom-call(bf16[2,64,2048]{2,1,0:T(8,128)(2,1)S(1)} %get-tuple-element.8.refs_0_, bf16[2,64,2048]{2,1,0:T(8,128)(2,1)S(1)} %get-tuple-element.9.refs_1_, bf16[2,64,2048]{2,1,0:T(8,128)(2,1)S(1)} %get-tuple-element.10.refs_2_, ...), custom_call_target="tpu_custom_call" | custom-call | tf_op jit(solution)/shard_map/hand_over/pallas_call | solution.py:468
